TPU v7x, 128 devices: a whole 4x4x4 slice. The times are simulated.
128 devices in a mesh: grp: 4 (over y), dev: 32 (over z, x, core).
Axes of the slice: x: 4, y: 4, z: 4, core: 2. Of those that a mesh axis runs over, the one named last changes fastest.
Arguments:
- points: float32 [3, 65536], P(None, 'dev'), may hold values from 0 to 1
- omega: bfloat16 [65536, 256], P('dev'), may hold values from -0.0234375 to 0.0234375
- pivots: int32 [32, 256], replicated, may hold values from 0 to 2047, as said below
- ranks: int32 [32], replicated, may hold values from 128 to 256, as said below
- owners: int32 [16], replicated, may hold values from 0 to 3, as said below
Outputs:
- interp: float32 [65536, 256], P(('grp', 'dev'))
- parent_samples: float32 [4, 8, 512, 256], P('grp', None, 'dev')
Inputs may be any that keep to these rules, and one draw needn't show every extreme that they name: The 256 pivots of a leaf are distinct. `ranks`: some leaf has exactly 256 skeleton rows in every draw. `owners`: no owner holds more than 8 parents, and some owner holds exactly 8.
All inputs are finite; a program needn't handle non-finite values.
Results may differ from a plain program's by a relative error of at most 0.0097.
Values may be sent and summed in bfloat16 or wider, within the bound.
A program may use at most 192 MiB of HBM per device.

v0:
```python
import math
import jax
import jax.numpy as jnp
from jax import lax
from jax.sharding import PartitionSpec as P

soften = 0.0001
highest = lax.Precision.HIGHEST


def copy_for_each(value, axis):
    copies = jnp.broadcast_to(value, (lax.axis_size(axis), *value.shape))
    return lax.all_to_all(copies, axis, split_axis=0, concat_axis=0, tiled=True)


def joined_along(parts, dim):
    parts = jnp.moveaxis(parts, 0, dim)
    lengths = parts.shape
    return parts.reshape(*lengths[:dim], lengths[dim] * lengths[dim + 1], *lengths[dim + 2 :])


def gathered_copies(value, axis, dim):
    parts = copy_for_each(value, axis)
    return joined_along(parts, dim)


def in_blocks(value, dim, peers):
    before, after = (value.shape[:dim], value.shape[dim + 1 :])
    return jnp.moveaxis(value.reshape(*before, peers, -1, *after), dim, 0)


def sum_at_owner(value, axis, dim):
    parts = in_blocks(value, dim, lax.axis_size(axis))
    arrived = lax.all_to_all(parts, axis, split_axis=0, concat_axis=0, tiled=True)
    return arrived.sum(axis=0)


def shifted(block, axis, distance):
    devices = range(lax.axis_size(axis))
    route = [(i - distance, i) for i in devices if i - distance in devices]
    return lax.ppermute(block, axis, route)


def kernel_block(row_pts, col_pts):
    dist_sq = (row_pts[0][:, None] - col_pts[0][None, :]) ** 2
    dist_sq = dist_sq + (row_pts[1][:, None] - col_pts[1][None, :]) ** 2
    dist_sq = dist_sq + (row_pts[2][:, None] - col_pts[2][None, :]) ** 2
    return 1.0 / jnp.sqrt(dist_sq + soften)


def body(points, omega, pivots, ranks, owners):
    groups = lax.axis_size("grp")
    devices = lax.axis_size("dev")
    group_id = lax.axis_index("grp")
    device_id = lax.axis_index("dev")
    leaf_size = omega.shape[0]
    samples_n = omega.shape[1]
    rank_max = pivots.shape[1]
    count_all = leaf_size * devices
    rows_group = count_all // groups
    slab_rows = leaf_size // groups
    leaves_group = devices // groups
    every_point = gathered_copies(points, "dev", 1)
    slab_start = group_id * rows_group + device_id * slab_rows
    my_leaf = slab_start // leaf_size
    slab_pts = lax.dynamic_slice_in_dim(every_point, slab_start, slab_rows, 1)
    start_sum = jnp.zeros((slab_rows, samples_n), jnp.float32)
    piece = lax.all_gather(omega, "dev", axis=0, tiled=True)
    piece_len = piece.shape[0]
    col_blk = math.gcd(piece_len, 2048)

    def one_block(number, running):
        first_col = number * col_blk
        col_pts = lax.dynamic_slice_in_dim(every_point, first_col, col_blk, 1)
        sketch = lax.dynamic_slice_in_dim(piece, number * col_blk, col_blk, 0)
        col_leaf = (first_col + jnp.arange(col_blk, dtype=jnp.int32)) // leaf_size
        kernel = kernel_block(slab_pts, col_pts)
        kernel = jnp.where(col_leaf[None, :] == my_leaf, 0.0, kernel).astype(jnp.bfloat16)
        return running + jnp.dot(kernel, sketch, preferred_element_type=jnp.float32)

    slab_samples = lax.fori_loop(0, piece_len // col_blk, one_block, start_sum)
    rank_ids = jnp.arange(rank_max, dtype=jnp.int32)
    local_leaf = device_id // groups
    within = slab_start - my_leaf * leaf_size
    my_pivots = pivots[my_leaf]
    my_live = rank_ids < ranks[my_leaf]
    slab_ids = jnp.arange(slab_rows, dtype=jnp.int32)
    picker = (my_pivots[:, None] - within == slab_ids[None, :]) & my_live[:, None]
    picked = jnp.dot(picker.astype(jnp.float32), slab_samples, precision=highest)
    sibling_leaf = jnp.bitwise_xor(device_id, 1)
    sib_pivots = pivots[sibling_leaf]
    sib_pts = every_point[:, sibling_leaf * leaf_size + sib_pivots]
    sib_kernel = kernel_block(sib_pts, points).astype(jnp.bfloat16)
    sib_live = (rank_ids < ranks[sibling_leaf]) & (device_id // leaves_group == group_id)
    correction = jnp.where(
        sib_live[:, None], jnp.dot(sib_kernel, omega, preferred_element_type=jnp.float32), 0.0
    )
    leaf_slots = jnp.arange(leaves_group, dtype=jnp.int32)
    skel_all = jnp.where((leaf_slots == local_leaf)[:, None, None], picked[None], 0.0)
    corr_all = jnp.where(
        (leaf_slots == sibling_leaf - group_id * leaves_group)[:, None, None], correction[None], 0.0
    )
    pairs_group = leaves_group // 2
    paired_part = (skel_all - corr_all).reshape(pairs_group, 2 * rank_max, samples_n)
    my_piece = sum_at_owner(paired_part, "dev", 1)
    position = device_id % groups
    skel_rows = picked
    for offset in range(1 - groups, groups):
        if offset != 0:
            arrived = shifted(picked, "dev", offset)
            source = position - offset
            skel_rows = skel_rows + jnp.where((source >= 0) & (source < groups), arrived, 0.0)
    gram_mat = jnp.dot(skel_rows, skel_rows.T, precision=highest)
    ridge_term = 0.1 * jnp.trace(gram_mat) / ranks[my_leaf].astype(jnp.float32) + 1e-06
    gram_mat = gram_mat + ridge_term * jnp.eye(rank_max, dtype=jnp.float32)
    factor = jnp.linalg.cholesky(gram_mat)
    right_side = jnp.dot(slab_samples, skel_rows.T, precision=highest)
    interp = jax.scipy.linalg.cho_solve((factor, True), right_side.T).T
    parent_count = owners.shape[0]
    slot_count = 2 * pairs_group
    parent_ids = jnp.arange(parent_count, dtype=jnp.int32)
    shared = owners[:, None] == owners[None, :]
    slot_of = jnp.sum(shared & (parent_ids[None, :] < parent_ids[:, None]), axis=1)
    slot_ids = jnp.arange(slot_count, dtype=jnp.int32)
    all_pieces = lax.all_gather(my_piece, "grp", axis=0, tiled=True)
    placing = (owners[None, :] == group_id) & (slot_ids[:, None] == slot_of[None, :])
    delivered = jnp.einsum(
        "sp,prk->srk", placing.astype(jnp.float32), all_pieces, precision=highest
    )
    return (interp, delivered[None])


def solution(mesh):
    placed = (P(None, "dev"), P("dev", None), P(), P(), P())
    return jax.shard_map(
        body,
        mesh=mesh,
        in_specs=placed,
        out_specs=(P(("grp", "dev"), None), P("grp", None, "dev", None)),
        check_vma=False,
    )
```

profile of v0, /device:TPU:33, one launch (start us, length us, event | category | flops | bytes accessed | tf_op | source)
XLA Modules:
  0.0 352.9 jit_solution(2332731837905459463)
XLA Ops:
  9.9 8.3 %all-to-all-start = ((f32[32,3,2048]{2,1,0:T(4,128)}), f32[32,3,2048]{2,1,0:T(4,128)S(1)}, u32[]{:S(2)}, u32[]{:S(2)}) async-start(f32[32,3,2048]{2,1,0:T(4,128)} %broadcast_in_dim.127), calls=%async_computation | async-start | bytes 2097152 | tf_op jit(solution)/shard_map/all_to_all | solution.py:13
  23.4 16.6 %all-to-all-done = f32[32,3,2048]{2,1,0:T(4,128)S(1)} async-done(((f32[32,3,2048]{2,1,0:T(4,128)}), f32[32,3,2048]{2,1,0:T(4,128)S(1)}, u32[]{:S(2)}, u32[]{:S(2)}) %all-to-all-start) | async-done | bytes 786464 | tf_op jit(solution)/shard_map/all_to_all | solution.py:13
  39.9 15.4 %copy.36 = f32[3,32,2048]{0,2,1:T(8,128)} copy(f32[3,32,2048]{2,0,1:T(4,128)S(1)} %bitcast.89) | data formatting | bytes 1572864 | tf_op jit(solution)/shard_map/transpose | solution.py:17
  55.3 20.0 %copy.38 = f32[3,65536]{1,0:T(4,128)S(1)} copy(f32[3,65536]{0,1:T(8,128)} %bitcast.84) | data formatting | bytes 1572864
  75.3 12.7 %gather_fusion = f32[256,3]{1,0:T(8,128)S(1)} fusion(f32[3,65536]{0,1:T(8,128)} %bitcast.85, s32[1024]{0:T(1024)S(1)} %pad_clamp_fusion), kind=kCustom, calls=%fused_computation | custom fusion | bytes 7168 | tf_op jit(solution)/shard_map/gather | solution.py:92
  89.4 41.9 %all-gather.2.cloned.1.call-done = bf16[65536,256]{1,0:T(8,128)(2,1)} async-done(((bf16[2048,256]{1,0:T(8,128)(2,1)}), bf16[65536,256]{1,0:T(8,128)(2,1)}) %all-gather.2.cloned.1.call-update) | async-done | bytes 33554448 | tf_op jit(solution)/shard_map/all_gather | solution.py:68
  131.2 98.0 %while.18 = (s32[]{:T(128)}, f32[512,256]{1,0:T(8,128)S(1)}, s32[]{:T(128)}, f32[3,512]{1,0:T(4,128)S(1)}, f32[3,65536]{1,0:T(4,128)S(1)}, /*index=5*/bf16[65536...) while((s32[]{:T(128)}, f32[512,256]{1,0:T(8,128)S(1)}, ...), condition=%wide.region_1.2_spmd.clone, body=%wide.region_0.1_spmd.clone.sunk | while | flops 548702208 | bytes 2193629 | solution.py:81
  131.4 3.0 fusion.72
  134.5 2.9 fusion.72
  137.6 2.9 fusion.72
  143.7 2.9 fusion.72
  146.7 2.9 fusion.72
  149.8 2.9 fusion.72
  155.9 2.9 fusion.72
  159.0 2.9 fusion.72
  165.1 2.9 fusion.72
  177.3 2.9 fusion.72
  180.4 2.9 fusion.72
  186.5 2.9 fusion.72
  198.8 2.9 fusion.72
  211.0 2.9 fusion.72
  220.2 2.9 fusion.72
  229.7 5.3 %collective-permute-start = (f32[256,256]{1,0:T(8,128)S(1)}, f32[256,256]{1,0:T(8,128)S(1)}, u32[]{:S(2)}, u32[]{:S(2)}) collective-permute-start(f32[256,256]{1,0:T(8,128)S(1)} %fusion.19), channel_id=1, source_target_pairs={{3,0},{4,1},{5,2},{6,3},{7,4},{8,5},{9,6},{10,7},{11,8},{12,9},{13... | collective-permute-start | bytes 786440 | tf_op jit(solution)/shard_map/ppermute | solution.py:41
  238.4 3.0 collective-permute-start.2
  251.5 6.3 %all-to-all-start.1 = ((f32[32,4,16,256]{3,2,1,0:T(8,128)}), f32[32,4,16,256]{3,2,1,0:T(8,128)S(1)}, u32[]{:S(2)}, u32[]{:S(2)}) async-start(f32[32,4,16,256]{3,2,1,0:T(8,128)} %copy.40), calls=%async_computation.1 | async-start | bytes 4194304 | tf_op jit(solution)/shard_map/all_to_all | solution.py:34
  259.1 6.1 %collective-permute-done.5 = f32[256,256]{1,0:T(8,128)} collective-permute-done((f32[256,256]{1,0:T(8,128)S(1)}, f32[256,256]{1,0:T(8,128)}, u32[]{:S(2)}, u32[]{:S(2)}) %collective-permute-start.5) | collective-permute-done | bytes 262176 | tf_op jit(solution)/shard_map/ppermute | solution.py:41
  269.1 11.7 %cholesky.49 = f32[128,128]{1,0:T(8,128)S(1)} custom-call(f32[128,128]{1,0:T(8,128)S(1)} %cholesky.115), custom_call_target="Cholesky" | custom-call | tf_op jit(solution)/shard_map/jit(cholesky)/cholesky | solution.py:116
  280.8 9.8 %custom-call.18 = f32[1,128,128]{1,2,0:T(8,128)S(1)} custom-call(f32[1,128,128]{2,1,0:T(8,128)S(1)} %get-tuple-element.261), custom_call_target="InvertDiagBlocksLowerTriangular" | custom-call | tf_op jit(solution)/shard_map/jit(cholesky)/cholesky | solution.py:116
  292.8 11.7 %cholesky.103 = f32[128,128]{1,0:T(8,128)S(1)} custom-call(f32[128,128]{1,0:T(8,128)S(1)} %convolution_subtract_fusion.1), custom_call_target="Cholesky" | custom-call | tf_op jit(solution)/shard_map/jit(cholesky)/cholesky | solution.py:116
  306.7 3.9 %while.17 = (s32[]{:T(128)}, f32[256,256]{1,0:T(8,128)S(1)}, s32[2,2]{1,0:T(2,128)S(1)}, f32[2,128,128]{2,1,0:T(8,128)S(1)}, s32[]{:T(128)}) while((s32[]{:T(128)}, f32[256,256]{1,0:T(8,128)S(1)}, s32[2,2]{1,0:T(2,128)S(1)}, f32[2,128,128]{2,1,0:T(8,128)S(1)}, s32[]{:T(128)}) %tuple.89), condition=%wide.while_cond, body=%wide.while_body.sunk | while | flops 2 | bytes 131181 | solution.py:118
  310.6 19.9 %custom-call.19 = f32[2,128,128]{1,2,0:T(8,128)S(1)} custom-call(f32[2,128,128]{2,1,0:T(8,128)S(1)} %get-tuple-element.165), custom_call_target="InvertDiagBlocksLowerTriangular" | custom-call | tf_op jit(solution)/shard_map/jit(_cho_solve)/triangular_solve | solution.py:118
  334.7 10.3 %all_gather.7 = f32[16,16,256]{2,1,0:T(8,128)S(1)} all-gather(f32[4,16,256]{2,1,0:T(8,128)S(1)} %reduce_sum.30), channel_id=1, replica_groups=mesh['grp'=4,'dev'=32] {'grp'}, dimensions={0}, use_global_device_ids=true | all-gather | bytes 327680 | tf_op jit(solution)/shard_map/all_gather | solution.py:125
  (198 shorter events, 91.6 us)
Async XLA Ops:
  7.2 16.2 %copy-start.3 = (f32[3,2048]{1,0:T(4,128)S(1)}, f32[3,2048]{1,0:T(4,128)}, u32[]{:S(2)}) copy-start(f32[3,2048]{1,0:T(4,128)} %param.7) | copy-start | bytes 73732
  7.2 11.5 %copy-start.4 = (s32[32]{0:T(128)S(1)}, s32[32]{0:T(128)}, u32[]{:S(2)}) copy-start(s32[32]{0:T(128)} %param.10) | copy-start | bytes 388
  7.2 15.4 %copy-start.5 = (s32[16]{0:T(128)S(1)}, s32[16]{0:T(128)}, u32[]{:S(2)}) copy-start(s32[16]{0:T(128)} %param.11) | copy-start | bytes 196
  7.2 124.0 %all-gather.2.cloned.1.call-start = ((), (), s32[]{:S(2)}) async-start(), calls=%async_computation.2 | async-start | bytes 34603008 | tf_op jit(solution)/shard_map/all_gather | solution.py:68
  9.9 30.0 %all-to-all-start = ((f32[32,3,2048]{2,1,0:T(4,128)}), f32[32,3,2048]{2,1,0:T(4,128)S(1)}, u32[]{:S(2)}, u32[]{:S(2)}) async-start(f32[32,3,2048]{2,1,0:T(4,128)} %broadcast_in_dim.127), calls=%async_computation | async-start | bytes 2097152 | tf_op jit(solution)/shard_map/all_to_all | solution.py:13
  131.2 103.8 %copy-start = (bf16[2048,256]{1,0:T(8,128)(2,1)S(1)}, bf16[2048,256]{1,0:T(8,128)(2,1)}, u32[]{:S(2)}) copy-start(bf16[2048,256]{1,0:T(8,128)(2,1)} %param.8) | copy-start | bytes 3145732
  229.7 17.2 %collective-permute-start = (f32[256,256]{1,0:T(8,128)S(1)}, f32[256,256]{1,0:T(8,128)S(1)}, u32[]{:S(2)}, u32[]{:S(2)}) collective-permute-start(f32[256,256]{1,0:T(8,128)S(1)} %fusion.19), channel_id=1, source_target_pairs={{3,0},{4,1},{5,2},{6,3},{7,4},{8,5},{9,6},{10,7},{11,8},{12,9},{13... | collective-permute-start | bytes 786440 | tf_op jit(solution)/shard_map/ppermute | solution.py:41
  236.0 21.9 %collective-permute-start.1 = (f32[256,256]{1,0:T(8,128)S(1)}, f32[256,256]{1,0:T(8,128)S(1)}, u32[]{:S(2)}, u32[]{:S(2)}) collective-permute-start(f32[256,256]{1,0:T(8,128)S(1)} %fusion.19), channel_id=1, source_target_pairs={{2,0},{3,1},{4,2},{5,3},{6,4},{7,5},{8,6},{9,7},{10,8},{11,9},{12,... | collective-permute-start | bytes 786440 | tf_op jit(solution)/shard_map/ppermute | solution.py:41
  238.4 19.4 %collective-permute-start.2 = (f32[256,256]{1,0:T(8,128)S(1)}, f32[256,256]{1,0:T(8,128)}, u32[]{:S(2)}, u32[]{:S(2)}) collective-permute-start(f32[256,256]{1,0:T(8,128)S(1)} %fusion.19), channel_id=1, source_target_pairs={{1,0},{2,1},{3,2},{4,3},{5,4},{6,5},{7,6},{8,7},{9,8},{10,9},{11,1... | collective-permute-start | bytes 786440 | tf_op jit(solution)/shard_map/ppermute | solution.py:41
  241.5 16.4 %collective-permute-start.3 = (f32[256,256]{1,0:T(8,128)S(1)}, f32[256,256]{1,0:T(8,128)}, u32[]{:S(2)}, u32[]{:S(2)}) collective-permute-start(f32[256,256]{1,0:T(8,128)S(1)} %fusion.19), channel_id=1, source_target_pairs={{0,1},{1,2},{2,3},{3,4},{4,5},{5,6},{6,7},{7,8},{8,9},{9,10},{10,1... | collective-permute-start | bytes 786440 | tf_op jit(solution)/shard_map/ppermute | solution.py:41
  244.0 15.1 %collective-permute-start.4 = (f32[256,256]{1,0:T(8,128)S(1)}, f32[256,256]{1,0:T(8,128)}, u32[]{:S(2)}, u32[]{:S(2)}) collective-permute-start(f32[256,256]{1,0:T(8,128)S(1)} %fusion.19), channel_id=1, source_target_pairs={{0,2},{1,3},{2,4},{3,5},{4,6},{5,7},{6,8},{7,9},{8,10},{9,11},{10,... | collective-permute-start | bytes 786440 | tf_op jit(solution)/shard_map/ppermute | solution.py:41
  246.8 18.4 %collective-permute-start.5 = (f32[256,256]{1,0:T(8,128)S(1)}, f32[256,256]{1,0:T(8,128)}, u32[]{:S(2)}, u32[]{:S(2)}) collective-permute-start(f32[256,256]{1,0:T(8,128)S(1)} %fusion.19), channel_id=1, source_target_pairs={{0,3},{1,4},{2,5},{3,6},{4,7},{5,8},{6,9},{7,10},{8,11},{9,12},{10... | collective-permute-start | bytes 786440 | tf_op jit(solution)/shard_map/ppermute | solution.py:41
  251.5 83.1 %all-to-all-start.1 = ((f32[32,4,16,256]{3,2,1,0:T(8,128)}), f32[32,4,16,256]{3,2,1,0:T(8,128)S(1)}, u32[]{:S(2)}, u32[]{:S(2)}) async-start(f32[32,4,16,256]{3,2,1,0:T(8,128)} %copy.40), calls=%async_computation.1 | async-start | bytes 4194304 | tf_op jit(solution)/shard_map/all_to_all | solution.py:34
  257.8 1.3 copy-start.2
  266.4 40.1 %copy-start.6 = (s32[2]{0:T(128)S(1)}, s32[2]{0:T(128)}, u32[]{:S(2)}) copy-start(s32[2]{0:T(128)} %iota_multiply_fusion) | copy-start | bytes 28
  268.4 0.7 copy-start.1
Sparse Core Ops, SparseCore 0:
  10.3 120.9 all-gather.1
where the time goes:
time: 355 us; the launch traced here: 353 us
  matrix products  100 us (28%)
  waiting for transfers between devices  66.5 us (19%)
  local copies, waits for them, and re-layouts  64.2 us (18%)
  other arithmetic  59.7 us (17%)
  starting transfers between devices  33.1 us (9%)
  between operations  17.2 us (5%)
  blocking collectives  10.3 us (3%)
    dot_general x32, matrix products, one_block(): return running + jnp.dot(kernel, sketch, preferred_element_type=jnp.float32)  92.2 us
    all_gather x1, waiting for transfers between devices, body(): piece = lax.all_gather(omega, 'dev', axis=0, tiled=True)  41.9 us
    another operation x6, other arithmetic, body(): factor = jnp.linalg.cholesky(gram_mat)  34 us
    unnamed x18, local copies, waits for them, and re-layouts  22.5 us
    another operation x3, other arithmetic, body(): interp = jax.scipy.linalg.cho_solve((factor, True), right_side.T).T  20.5 us
    ppermute x6, starting transfers between devices, shifted(): return lax.ppermute(block, axis, route)  18.5 us
    all_to_all x1, waiting for transfers between devices, copy_for_each(): return lax.all_to_all(copies, axis, split_axis=0, concat_axis=0, tiled=True)  16.6 us
    transpose x1, local copies, waits for them, and re-layouts, joined_along(): parts = jnp.moveaxis(parts, 0, dim)  15.4 us
  transfers between devices with their start and end apart: 9, of which 4 were waited for; matrix products, arithmetic and copies ran while one was open for 36% of the time, Pallas kernels for 0%

commit v1 on v0

--- a/solution.py
+++ b/solution.py
@@ -65,7 +65,9 @@
     my_leaf = slab_start // leaf_size
     slab_pts = lax.dynamic_slice_in_dim(every_point, slab_start, slab_rows, 1)
     start_sum = jnp.zeros((slab_rows, samples_n), jnp.float32)
-    piece = lax.all_gather(omega, "dev", axis=0, tiled=True)
+    piece = jnp.concatenate(
+        lax.all_to_all(jnp.stack([omega] * lax.axis_size("dev")), "dev", 0, 0), axis=0
+    )
     piece_len = piece.shape[0]
     col_blk = math.gcd(piece_len, 2048)
 

time: 355 us -> 699 us (1.97); the launches traced: 353 us -> 690 us
  waiting for transfers between devices: 66.5 us -> 352 us
  starting transfers between devices: 33.1 us -> 64.2 us
  blocking collectives: 10.3 us -> 34.1 us
  between operations: 17.2 us -> 3.83 us
  local copies, waits for them, and re-layouts: 64.2 us -> 73 us
    all_to_all x1, waiting for transfers between devices: 16.6 us -> 352 us  [body(): lax.all_to_all(jnp.stack([omega] * lax.axis_size('dev')), 'dev', 0, 0)]
    all_gather x1 -> x0, waiting for transfers between devices: 41.9 us -> none  [body(): piece = lax.all_gather(omega, 'dev', axis=0, tiled=True)]
    ppermute x6, starting transfers between devices: 18.5 us -> 47.8 us  [shifted(): return lax.ppermute(block, axis, route)]
    all_to_all x0 -> x1, blocking collectives: none -> 23.7 us  [copy_for_each(): return lax.all_to_all(copies, axis, split_axis=0, concat_axis=0, tiled=True)]
    another operation x6 -> x7, local copies, waits for them, and re-layouts: 3.9 us -> 16.1 us  [the longest x1 10.9 us: body(): jnp.stack([omega] * lax.axis_size('dev'))]
    ppermute x6, waiting for transfers between devices: 7.35 us -> 0.02 us  [shifted(): return lax.ppermute(block, axis, route)]
    unnamed x18 -> x14, local copies, waits for them, and re-layouts: 22.5 us -> 20.5 us
  transfers between devices with their start and end apart: 9 -> 8, of which waited for: 4 -> 1; matrix products, arithmetic and copies ran while one was open for 36% -> 18% of each run, Pallas kernels for 0% -> 0%
where the time goes in v1:
time: 699 us; the launch traced here: 690 us
  waiting for transfers between devices  352 us (50%)
  matrix products  100 us (14%)
  local copies, waits for them, and re-layouts  73 us (10%)
  starting transfers between devices  64.2 us (9%)
  other arithmetic  60.5 us (9%)
  blocking collectives  34.1 us (5%)
    all_to_all x1, waiting for transfers between devices, body(): lax.all_to_all(jnp.stack([omega] * lax.axis_size('dev')), 'dev', 0, 0)  352 us
    dot_general x32, matrix products, one_block(): return running + jnp.dot(kernel, sketch, preferred_element_type=jnp.float32)  92.1 us
    ppermute x6, starting transfers between devices, shifted(): return lax.ppermute(block, axis, route)  47.8 us
    another operation x6, other arithmetic, body(): factor = jnp.linalg.cholesky(gram_mat)  34 us
    all_to_all x1, blocking collectives, copy_for_each(): return lax.all_to_all(copies, axis, split_axis=0, concat_axis=0, tiled=True)  23.7 us
    another operation x3, other arithmetic, body(): interp = jax.scipy.linalg.cho_solve((factor, True), right_side.T).T  20.5 us
    unnamed x14, local copies, waits for them, and re-layouts  20.5 us
    transpose x1, local copies, waits for them, and re-layouts, joined_along(): parts = jnp.moveaxis(parts, 0, dim)  15.4 us
  transfers between devices with their start and end apart: 8, of which 1 were waited for; matrix products, arithmetic and copies ran while one was open for 18% of the time, Pallas kernels for 0%

profile of v1, /device:TPU:33, one launch (start us, length us, event | category | flops | bytes accessed | tf_op | source)
XLA Modules:
  0.0 689.9 jit_solution(16369430782688764849)
XLA Ops:
  1.7 23.7 %all_to_all.15 = f32[32,3,2048]{2,1,0:T(4,128)S(1)} all-to-all(f32[32,3,2048]{2,1,0:T(4,128)S(1)} %broadcast_in_dim.127), channel_id=1, replica_groups=mesh['grp'=4,'dev'=32] {'dev'}, dimensions={0} | all-to-all | bytes 1572864 | tf_op jit(solution)/shard_map/all_to_all | solution.py:13
  25.4 10.9 %stack.2 = bf16[32,2048,256]{2,1,0:T(8,128)(2,1)} broadcast(bf16[2048,256]{1,0:T(8,128)(2,1)S(1)} %copy-done), dimensions={1,2} | broadcast | bytes 34603008 | tf_op jit(solution)/shard_map/stack | solution.py:69
  36.3 7.3 %all-to-all-start.1 = ((bf16[32,2048,256]{2,1,0:T(8,128)(2,1)}), bf16[32,2048,256]{2,1,0:T(8,128)(2,1)}, u32[]{:S(2)}, u32[]{:S(2)}) async-start(bf16[32,2048,256]{2,1,0:T(8,128)(2,1)} %stack.2), calls=%async_computation.1 | async-start | bytes 67108864 | tf_op jit(solution)/shard_map/all_to_all | solution.py:69
  48.4 15.4 %copy.36 = f32[3,32,2048]{0,2,1:T(8,128)} copy(f32[3,32,2048]{2,0,1:T(4,128)S(1)} %bitcast.90) | data formatting | bytes 1572864 | tf_op jit(solution)/shard_map/transpose | solution.py:17
  63.8 18.0 %copy.38 = f32[3,65536]{1,0:T(4,128)S(1)} copy(f32[3,65536]{0,1:T(8,128)} %bitcast.85) | data formatting | bytes 1572864
  81.8 11.3 %gather_fusion = f32[256,3]{1,0:T(8,128)S(1)} fusion(f32[3,65536]{0,1:T(8,128)} %bitcast.86, s32[1024]{0:T(1024)S(1)} %pad_clamp_fusion), kind=kCustom, calls=%fused_computation | custom fusion | bytes 7168 | tf_op jit(solution)/shard_map/gather | solution.py:94
  94.4 352.5 %all-to-all-done.1 = bf16[32,2048,256]{2,1,0:T(8,128)(2,1)} async-done(((bf16[32,2048,256]{2,1,0:T(8,128)(2,1)}), bf16[32,2048,256]{2,1,0:T(8,128)(2,1)}, u32[]{:S(2)}, u32[]{:S(2)}) %all-to-all-start.1) | async-done | bytes 33554464 | tf_op jit(solution)/shard_map/all_to_all | solution.py:69
  446.9 97.9 %while.18 = (s32[]{:T(128)}, f32[512,256]{1,0:T(8,128)S(1)}, s32[]{:T(128)}, f32[3,512]{1,0:T(4,128)S(1)}, f32[3,65536]{1,0:T(4,128)S(1)}, /*index=5*/bf16[65536...) while((s32[]{:T(128)}, f32[512,256]{1,0:T(8,128)S(1)}, ...), condition=%wide.region_1.2_spmd.clone, body=%wide.region_0.1_spmd.clone.sunk | while | flops 548702208 | bytes 2193629 | solution.py:83
  453.2 2.9 fusion.72
  456.2 2.9 fusion.72
  462.4 2.9 fusion.72
  465.4 2.9 fusion.72
  474.6 2.9 fusion.72
  477.6 2.9 fusion.72
  483.8 2.9 fusion.72
  496.0 2.9 fusion.72
  505.2 2.9 fusion.72
  517.4 2.9 fusion.72
  529.7 2.9 fusion.72
  541.9 2.9 fusion.72
  545.3 22.6 %collective-permute-start = (f32[256,256]{1,0:T(8,128)S(1)}, f32[256,256]{1,0:T(8,128)S(1)}, u32[]{:S(2)}, u32[]{:S(2)}) collective-permute-start(f32[256,256]{1,0:T(8,128)S(1)} %fusion.19), channel_id=1, source_target_pairs={{3,0},{4,1},{5,2},{6,3},{7,4},{8,5},{9,6},{10,7},{11,8},{12,9},{13... | collective-permute-start | bytes 786440 | tf_op jit(solution)/shard_map/ppermute | solution.py:41
  568.8 4.6 collective-permute-start.1
  575.3 3.6 collective-permute-start.3
  578.9 10.3 %collective-permute-start.4 = (f32[256,256]{1,0:T(8,128)S(1)}, f32[256,256]{1,0:T(8,128)}, u32[]{:S(2)}, u32[]{:S(2)}) collective-permute-start(f32[256,256]{1,0:T(8,128)S(1)} %fusion.19), channel_id=1, source_target_pairs={{0,2},{1,3},{2,4},{3,5},{4,6},{5,7},{6,8},{7,9},{8,10},{9,11},{10,... | collective-permute-start | bytes 786440 | tf_op jit(solution)/shard_map/ppermute | solution.py:41
  589.3 4.7 collective-permute-start.5
  596.4 9.2 %all-to-all-start.2 = ((f32[32,4,16,256]{3,2,1,0:T(8,128)}), f32[32,4,16,256]{3,2,1,0:T(8,128)S(1)}, u32[]{:S(2)}, u32[]{:S(2)}) async-start(f32[32,4,16,256]{3,2,1,0:T(8,128)} %copy.40), calls=%async_computation.2 | async-start | bytes 4194304 | tf_op jit(solution)/shard_map/all_to_all | solution.py:34
  611.0 11.7 %cholesky.49 = f32[128,128]{1,0:T(8,128)S(1)} custom-call(f32[128,128]{1,0:T(8,128)S(1)} %cholesky.115), custom_call_target="Cholesky" | custom-call | tf_op jit(solution)/shard_map/jit(cholesky)/cholesky | solution.py:118
  622.8 9.8 %custom-call.18 = f32[1,128,128]{1,2,0:T(8,128)S(1)} custom-call(f32[1,128,128]{2,1,0:T(8,128)S(1)} %get-tuple-element.261), custom_call_target="InvertDiagBlocksLowerTriangular" | custom-call | tf_op jit(solution)/shard_map/jit(cholesky)/cholesky | solution.py:118
  634.8 11.7 %cholesky.103 = f32[128,128]{1,0:T(8,128)S(1)} custom-call(f32[128,128]{1,0:T(8,128)S(1)} %convolution_subtract_fusion.1), custom_call_target="Cholesky" | custom-call | tf_op jit(solution)/shard_map/jit(cholesky)/cholesky | solution.py:118
  648.5 5.2 while.17
  653.7 20.5 %custom-call.19 = f32[2,128,128]{1,2,0:T(8,128)S(1)} custom-call(f32[2,128,128]{2,1,0:T(8,128)} %get-tuple-element.165), custom_call_target="InvertDiagBlocksLowerTriangular" | custom-call | tf_op jit(solution)/shard_map/jit(_cho_solve)/triangular_solve | solution.py:120
  678.4 10.4 %all_gather.3 = f32[16,16,256]{2,1,0:T(8,128)S(1)} all-gather(f32[4,16,256]{2,1,0:T(8,128)S(1)} %reduce_sum.30), channel_id=1, replica_groups=mesh['grp'=4,'dev'=32] {'grp'}, dimensions={0}, use_global_device_ids=true | all-gather | bytes 327680 | tf_op jit(solution)/shard_map/all_gather | solution.py:127
  (193 shorter events, 91.6 us)
Async XLA Ops:
  0.6 24.8 %copy-start = (bf16[2048,256]{1,0:T(8,128)(2,1)S(1)}, bf16[2048,256]{1,0:T(8,128)(2,1)}, u32[]{:S(2)}) copy-start(bf16[2048,256]{1,0:T(8,128)(2,1)} %param.8) | copy-start | bytes 3145732
  36.3 7.8 %copy-start.3 = (s32[32]{0:T(128)S(1)}, s32[32]{0:T(128)}, u32[]{:S(2)}) copy-start(s32[32]{0:T(128)} %param.10) | copy-start | bytes 388
  36.3 11.9 %copy-start.4 = (s32[16]{0:T(128)S(1)}, s32[16]{0:T(128)}, u32[]{:S(2)}) copy-start(s32[16]{0:T(128)} %param.11) | copy-start | bytes 196
  36.3 12.1 %copy-start.2 = (f32[3,2048]{1,0:T(4,128)S(1)}, f32[3,2048]{1,0:T(4,128)}, u32[]{:S(2)}) copy-start(f32[3,2048]{1,0:T(4,128)} %param.7) | copy-start | bytes 73732
  36.3 410.6 %all-to-all-start.1 = ((bf16[32,2048,256]{2,1,0:T(8,128)(2,1)}), bf16[32,2048,256]{2,1,0:T(8,128)(2,1)}, u32[]{:S(2)}, u32[]{:S(2)}) async-start(bf16[32,2048,256]{2,1,0:T(8,128)(2,1)} %stack.2), calls=%async_computation.1 | async-start | bytes 67108864 | tf_op jit(solution)/shard_map/all_to_all | solution.py:69
  545.3 44.0 %collective-permute-start = (f32[256,256]{1,0:T(8,128)S(1)}, f32[256,256]{1,0:T(8,128)S(1)}, u32[]{:S(2)}, u32[]{:S(2)}) collective-permute-start(f32[256,256]{1,0:T(8,128)S(1)} %fusion.19), channel_id=1, source_target_pairs={{3,0},{4,1},{5,2},{6,3},{7,4},{8,5},{9,6},{10,7},{11,8},{12,9},{13... | collective-permute-start | bytes 786440 | tf_op jit(solution)/shard_map/ppermute | solution.py:41
  568.8 36.8 %collective-permute-start.1 = (f32[256,256]{1,0:T(8,128)S(1)}, f32[256,256]{1,0:T(8,128)S(1)}, u32[]{:S(2)}, u32[]{:S(2)}) collective-permute-start(f32[256,256]{1,0:T(8,128)S(1)} %fusion.19), channel_id=1, source_target_pairs={{2,0},{3,1},{4,2},{5,3},{6,4},{7,5},{8,6},{9,7},{10,8},{11,9},{12,... | collective-permute-start | bytes 786440 | tf_op jit(solution)/shard_map/ppermute | solution.py:41
  573.4 32.3 %collective-permute-start.2 = (f32[256,256]{1,0:T(8,128)S(1)}, f32[256,256]{1,0:T(8,128)}, u32[]{:S(2)}, u32[]{:S(2)}) collective-permute-start(f32[256,256]{1,0:T(8,128)S(1)} %fusion.19), channel_id=1, source_target_pairs={{1,0},{2,1},{3,2},{4,3},{5,4},{6,5},{7,6},{8,7},{9,8},{10,9},{11,1... | collective-permute-start | bytes 786440 | tf_op jit(solution)/shard_map/ppermute | solution.py:41
  575.3 30.3 %collective-permute-start.3 = (f32[256,256]{1,0:T(8,128)S(1)}, f32[256,256]{1,0:T(8,128)}, u32[]{:S(2)}, u32[]{:S(2)}) collective-permute-start(f32[256,256]{1,0:T(8,128)S(1)} %fusion.19), channel_id=1, source_target_pairs={{0,1},{1,2},{2,3},{3,4},{4,5},{5,6},{6,7},{7,8},{8,9},{9,10},{10,1... | collective-permute-start | bytes 786440 | tf_op jit(solution)/shard_map/ppermute | solution.py:41
  578.9 26.7 %collective-permute-start.4 = (f32[256,256]{1,0:T(8,128)S(1)}, f32[256,256]{1,0:T(8,128)}, u32[]{:S(2)}, u32[]{:S(2)}) collective-permute-start(f32[256,256]{1,0:T(8,128)S(1)} %fusion.19), channel_id=1, source_target_pairs={{0,2},{1,3},{2,4},{3,5},{4,6},{5,7},{6,8},{7,9},{8,10},{9,11},{10,... | collective-permute-start | bytes 786440 | tf_op jit(solution)/shard_map/ppermute | solution.py:41
  589.3 17.0 %collective-permute-start.5 = (f32[256,256]{1,0:T(8,128)S(1)}, f32[256,256]{1,0:T(8,128)}, u32[]{:S(2)}, u32[]{:S(2)}) collective-permute-start(f32[256,256]{1,0:T(8,128)S(1)} %fusion.19), channel_id=1, source_target_pairs={{0,3},{1,4},{2,5},{3,6},{4,7},{5,8},{6,9},{7,10},{8,11},{9,12},{10... | collective-permute-start | bytes 786440 | tf_op jit(solution)/shard_map/ppermute | solution.py:41
  596.4 81.9 %all-to-all-start.2 = ((f32[32,4,16,256]{3,2,1,0:T(8,128)}), f32[32,4,16,256]{3,2,1,0:T(8,128)S(1)}, u32[]{:S(2)}, u32[]{:S(2)}) async-start(f32[32,4,16,256]{3,2,1,0:T(8,128)} %copy.40), calls=%async_computation.2 | async-start | bytes 4194304 | tf_op jit(solution)/shard_map/all_to_all | solution.py:34
  605.6 0.7 copy-start.1
